TPU v7x, 256 devices: a whole 4x4x8 slice. The times are simulated.
256 devices in a mesh: fsdp: 16 (over y, x), ep: 16 (over z, core).
Axes of the slice: x: 4, y: 4, z: 8, core: 2. Of those that a mesh axis runs over, the one named last changes fastest.
Arguments:
- tokens: bfloat16 [8192, 7168], P('ep', 'fsdp'), may hold values from -6 to 6
- cotangent: bfloat16 [8192, 7168], P('ep', 'fsdp'), may hold values from -3 to 3
- gate_weight: bfloat16 [16, 7168, 2048], P('ep', None, 'fsdp'), may hold values from -0.0625 to 0.0625
- up_weight: bfloat16 [16, 7168, 2048], P('ep', None, 'fsdp'), may hold values from -0.0625 to 0.0625
- down_weight: bfloat16 [16, 2048, 7168], P('ep', 'fsdp'), may hold values from -0.125 to 0.125
- chosen: int32 [16, 16, 16], P(None, 'ep'), may hold values from 0 to 511, as said below
- counts: int32 [16, 16], P(None, 'ep'), may hold values from 1 to 16, as said below
- gate_prob: float32 [16, 16, 16], P(None, 'ep'), may hold values from 0.2 to 1
Outputs:
- mixture: bfloat16 [8192, 7168], P('ep', 'fsdp')
- grad_tokens: bfloat16 [8192, 7168], P('ep', 'fsdp')
- grad_gate: bfloat16 [16, 7168, 2048], P('ep', None, 'fsdp')
- grad_up: bfloat16 [16, 7168, 2048], P('ep', None, 'fsdp')
- grad_down: bfloat16 [16, 2048, 7168], P('ep', 'fsdp')
Inputs may be any that keep to these rules, and one draw needn't show every extreme that they name: For each expert e and group s the entries chosen[e, s, j] with j < counts[e, s] are distinct; the remaining entries are padding. `counts`: in every draw one expert takes 16 rows from every group.
All inputs are finite; a program needn't handle non-finite values.
Results may differ from a plain program's by a relative error of at most 0.017.
Values may be sent and summed in bfloat16 or wider, within the bound.
A program may use at most 192 MiB of HBM per device.

v0:
```python
import jax
import jax.numpy as jnp
from jax import lax
from jax.sharding import PartitionSpec as P


def pick_rows(tokens, cotangent, row_index, live_mask, weight):
    flat_rows = row_index.reshape(-1)
    keep_rows = live_mask.reshape(-1)[:, None]
    taken_tokens = jnp.take(tokens, flat_rows, axis=0)
    picked_tokens = jnp.where(keep_rows, taken_tokens, jnp.zeros_like(taken_tokens))
    taken_grads = jnp.take(cotangent, flat_rows, axis=0).astype(jnp.float32)
    picked_grads = (weight.reshape(-1)[:, None] * taken_grads).astype(jnp.bfloat16)
    shaped = row_index.shape + (tokens.shape[1],)
    return (picked_tokens.reshape(shaped), picked_grads.reshape(shaped))


def to_slots(summed, experts, slot_count):
    return summed.astype(jnp.bfloat16).reshape(experts, slot_count, summed.shape[1])


def send_back(term, experts, slot_count):
    summed = lax.psum_scatter(
        term.astype(jnp.bfloat16), "fsdp", scatter_dimension=1, tiled=True
    ).astype(jnp.float32)
    return lax.all_to_all(
        to_slots(summed, experts, slot_count), "ep", split_axis=0, concat_axis=0, tiled=True
    )


def per_device(tokens, cotangent, gate_weight, up_weight, down_weight, chosen, counts, gate_prob):
    experts = chosen.shape[0]
    slot_count = chosen.shape[2]
    features = tokens.shape[1]
    row_index = chosen[:, 0, :]
    position = lax.broadcasted_iota(jnp.int32, (experts, slot_count), 1)
    live_mask = position < counts
    weight = jnp.where(live_mask, gate_prob[:, 0, :], 0.0)
    picked_tokens, picked_grads = pick_rows(tokens, cotangent, row_index, live_mask, weight)
    wide_tokens, wide_grads = (
        lax.all_gather(picked_tokens, "fsdp", axis=2, tiled=True),
        lax.all_gather(picked_grads, "fsdp", axis=2, tiled=True),
    )
    rows_tokens, rows_grads = (
        lax.all_to_all(wide_tokens, "ep", split_axis=0, concat_axis=0, tiled=True),
        lax.all_to_all(wide_grads, "ep", split_axis=0, concat_axis=0, tiled=True),
    )
    full_width = rows_tokens.shape[2]
    total_rows = rows_tokens.shape[0] * slot_count
    rows_tokens = rows_tokens.reshape(total_rows, full_width)
    rows_grads = rows_grads.reshape(total_rows, full_width)
    gate_local = gate_weight[0]
    up_local = up_weight[0]
    down_local = down_weight[0]
    pre_gate = jnp.dot(rows_tokens, gate_local, preferred_element_type=jnp.float32)
    pre_up = jnp.dot(rows_tokens, up_local, preferred_element_type=jnp.float32)
    sigmoid_gate = jax.nn.sigmoid(pre_gate)
    activated = pre_gate * sigmoid_gate
    hidden = (activated * pre_up).astype(jnp.bfloat16)
    output_term = jnp.dot(hidden, down_local, preferred_element_type=jnp.float32)
    output_back = send_back(output_term, experts, slot_count)
    contract_rows = (((0,), (0,)), ((), ()))
    contract_last = (((1,), (1,)), ((), ()))
    grad_hidden = lax.dot_general(
        rows_grads, down_local, contract_last, preferred_element_type=jnp.float32
    )
    grad_pre_gate = (
        grad_hidden * pre_up * sigmoid_gate * (1.0 + pre_gate * (1.0 - sigmoid_gate))
    ).astype(jnp.bfloat16)
    grad_pre_up = (grad_hidden * activated).astype(jnp.bfloat16)
    grad_down = lax.dot_general(
        hidden, rows_grads, contract_rows, preferred_element_type=jnp.float32
    ).astype(jnp.bfloat16)
    grad_gate = lax.dot_general(
        rows_tokens, grad_pre_gate, contract_rows, preferred_element_type=jnp.float32
    ).astype(jnp.bfloat16)
    grad_up = lax.dot_general(
        rows_tokens, grad_pre_up, contract_rows, preferred_element_type=jnp.float32
    ).astype(jnp.bfloat16)
    grad_term = lax.dot_general(
        grad_pre_gate, gate_local, contract_last, preferred_element_type=jnp.float32
    )
    grad_term = grad_term + lax.dot_general(
        grad_pre_up, up_local, contract_last, preferred_element_type=jnp.float32
    )
    grad_back = send_back(grad_term, experts, slot_count)
    flat_rows = row_index.reshape(-1)
    output_rows = output_back.reshape(-1, features).astype(jnp.float32)
    mixture = (
        jnp.zeros((tokens.shape[0], features), jnp.float32)
        .at[flat_rows]
        .add(weight.reshape(-1)[:, None] * output_rows)
    )
    grad_rows = jnp.where(
        live_mask.reshape(-1)[:, None], grad_back.reshape(-1, features).astype(jnp.float32), 0.0
    )
    grad_tokens = jnp.zeros((tokens.shape[0], features), jnp.float32).at[flat_rows].add(grad_rows)
    return (
        mixture.astype(jnp.bfloat16),
        grad_tokens.astype(jnp.bfloat16),
        grad_gate[None],
        grad_up[None],
        grad_down[None],
    )


def solution(mesh):
    placed = (
        P("ep", "fsdp"),
        P("ep", "fsdp"),
        P("ep", None, "fsdp"),
        P("ep", None, "fsdp"),
        P("ep", "fsdp", None),
        P(None, "ep", None),
        P(None, "ep"),
        P(None, "ep", None),
    )
    return jax.shard_map(
        per_device,
        mesh=mesh,
        in_specs=placed,
        out_specs=(
            P("ep", "fsdp"),
            P("ep", "fsdp"),
            P("ep", None, "fsdp"),
            P("ep", None, "fsdp"),
            P("ep", "fsdp", None),
        ),
        check_vma=False,
    )
```

profile of v0, /device:TPU:1, one launch (start us, length us, event | category | flops | bytes accessed | tf_op | source)
XLA Modules:
  0.0 701.6 jit_solution(7673215205043818833)
XLA Ops:
  7.2 0.9 reshape_squeeze.7
  8.1 0.7 iota_compare_fusion
  8.9 0.1 lt.41
  9.0 1.2 copy.31
  10.2 1.2 gather_fusion
  11.4 0.1 select_select_fusion
  11.5 1.9 copy.32
  13.5 0.0 all-gather.5.cloned.1.call-start
  13.5 0.5 broadcast.74
  14.0 0.7 reduce.9
  14.7 0.1 squeeze.12
  14.8 0.2 copy.35
  15.0 1.2 gather_fusion.1
  16.2 0.1 multiply_convert_fusion
  16.3 1.9 copy.36
  18.3 179.5 %all-gather.3.cloned.1.call-done = bf16[16,16,7168]{1,0,2:T(8,128)(2,1)} async-done(((bf16[16,16,448]{1,0,2:T(8,128)(2,1)}), bf16[16,16,7168]{1,0,2:T(8,128)(2,1)}) %all-gather.3.cloned.1.call-update) | async-done | bytes 3670032 | tf_op jit(solution)/shard_map/all_gather | solution.py:41
  197.8 26.9 %copy.33 = bf16[16,16,7168]{2,1,0:T(8,128)(2,1)} copy(bf16[16,16,7168]{1,0,2:T(8,128)(2,1)} %all-gather.3.cloned.1.call-done) | data formatting | bytes 7340032 | tf_op jit(solution)/shard_map/all_gather | solution.py:41
  224.7 7.9 %all-to-all-start = ((bf16[16,16,7168]{2,1,0:T(8,128)(2,1)}), bf16[16,16,7168]{2,1,0:T(8,128)(2,1)}, u32[]{:S(2)}, u32[]{:S(2)}) async-start(bf16[16,16,7168]{2,1,0:T(8,128)(2,1)} %copy.33), calls=%async_computation | async-start | bytes 7340032 | tf_op jit(solution)/shard_map/all_to_all | solution.py:45
  232.6 148.5 %all-gather.5.cloned.1.call-done = bf16[16,16,7168]{1,0,2:T(8,128)(2,1)} async-done(((bf16[16,16,448]{1,0,2:T(8,128)(2,1)}), bf16[16,16,7168]{1,0,2:T(8,128)(2,1)}) %all-gather.5.cloned.1.call-update) | async-done | bytes 3670032 | tf_op jit(solution)/shard_map/all_gather | solution.py:42
  381.1 26.5 %copy.37 = bf16[16,16,7168]{2,1,0:T(8,128)(2,1)} copy(bf16[16,16,7168]{1,0,2:T(8,128)(2,1)} %all-gather.5.cloned.1.call-done) | data formatting | bytes 7340032 | tf_op jit(solution)/shard_map/all_gather | solution.py:42
  407.6 7.9 %all-to-all-start.2 = ((bf16[16,16,7168]{2,1,0:T(8,128)(2,1)}), bf16[16,16,7168]{2,1,0:T(8,128)(2,1)}, u32[]{:S(2)}, u32[]{:S(2)}) async-start(bf16[16,16,7168]{2,1,0:T(8,128)(2,1)} %copy.37), calls=%async_computation.3 | async-start | bytes 7340032 | tf_op jit(solution)/shard_map/all_to_all | solution.py:46
  415.5 3.8 fusion.8
  419.4 3.2 fusion.12
  422.6 75.2 %all-to-all-done.2 = bf16[16,16,7168]{2,1,0:T(8,128)(2,1)} async-done(((bf16[16,16,7168]{2,1,0:T(8,128)(2,1)}), bf16[16,16,7168]{2,1,0:T(8,128)(2,1)}, u32[]{:S(2)}, u32[]{:S(2)}) %all-to-all-start.2) | async-done | bytes 3670048 | tf_op jit(solution)/shard_map/all_to_all | solution.py:46
  497.7 3.2 multiply_convert_fusion.1
  500.9 3.1 convolution_convert_fusion
  504.0 0.0 reduce-scatter.5.cloned.1.call-start
  504.1 2.7 fusion.10
  506.8 2.9 fusion
  509.8 0.5 broadcast.73
  510.3 0.2 copy-done.4
  510.5 0.7 reduce.8
  511.1 0.1 reshape_squeeze.6
  511.2 71.2 %reduce-scatter.3.cloned.1.call-done = bf16[256,448]{0,1:T(8,128)(2,1)} async-done(((bf16[256,7168]{0,1:T(8,128)(2,1)}), bf16[256,448]{0,1:T(8,128)(2,1)}) %reduce-scatter.3.cloned.1.call-update) | async-done | bytes 229392 | tf_op jit(solution)/shard_map/reduce_scatter | solution.py:23
  582.4 1.8 copy.34
  584.2 9.4 %all-to-all-start.1 = ((bf16[16,16,448]{2,1,0:T(8,128)(2,1)}), bf16[16,16,448]{2,1,0:T(8,128)(2,1)S(1)}, u32[]{:S(2)}, u32[]{:S(2)}) async-start(bf16[16,16,448]{2,1,0:T(8,128)(2,1)} %bitcast.7), calls=%async_computation.2 | async-start | bytes 524288 | tf_op jit(solution)/shard_map/all_to_all | solution.py:26
  593.6 3.9 fusion.3
  597.5 70.1 %reduce-scatter.5.cloned.1.call-done = bf16[256,448]{0,1:T(8,128)(2,1)} async-done(((bf16[256,7168]{0,1:T(8,128)(2,1)}), bf16[256,448]{0,1:T(8,128)(2,1)}) %reduce-scatter.5.cloned.1.call-update) | async-done | bytes 229392 | tf_op jit(solution)/shard_map/reduce_scatter | solution.py:23
  667.6 1.8 copy.38
  669.4 9.4 %all-to-all-start.3 = ((bf16[16,16,448]{2,1,0:T(8,128)(2,1)}), bf16[16,16,448]{2,1,0:T(8,128)(2,1)}, u32[]{:S(2)}, u32[]{:S(2)}) async-start(bf16[16,16,448]{2,1,0:T(8,128)(2,1)} %bitcast.11), calls=%async_computation.5 | async-start | bytes 524288 | tf_op jit(solution)/shard_map/all_to_all | solution.py:26
  678.8 4.4 fusion.2
  683.2 4.4 fusion.1
  687.6 2.4 scatter_custom_fusion
  690.1 0.1 convert_element_type.56
  690.2 1.0 copy.39
  691.1 2.8 scatter_custom_fusion.1
  694.0 0.1 convert_element_type.64
  694.1 1.0 copy.40
  (25 shorter events, 0.2 us)
Async XLA Ops:
  7.2 490.6 %copy-start = (bf16[1,128,7168]{2,1,0:T(8,128)(2,1)S(1)}, bf16[1,128,7168]{2,1,0:T(8,128)(2,1)}, u32[]{:S(2)}) copy-start(bf16[1,128,7168]{2,1,0:T(8,128)(2,1)} %param.14) | copy-start | bytes 5505028
  7.2 190.6 %all-gather.3.cloned.1.call-start = ((), (), s32[]{:S(2)}) async-start(), calls=%async_computation.6 | async-start | bytes 31195136 | tf_op jit(solution)/shard_map/all_gather | solution.py:41
  9.0 5.1 copy-start.5
  10.2 4.6 copy-start.3
  13.5 367.6 %all-gather.5.cloned.1.call-start = ((), (), s32[]{:S(2)}) async-start(), calls=%async_computation.8 | async-start | bytes 31195136 | tf_op jit(solution)/shard_map/all_gather | solution.py:42
  224.7 182.9 %all-to-all-start = ((bf16[16,16,7168]{2,1,0:T(8,128)(2,1)}), bf16[16,16,7168]{2,1,0:T(8,128)(2,1)}, u32[]{:S(2)}, u32[]{:S(2)}) async-start(bf16[16,16,7168]{2,1,0:T(8,128)(2,1)} %copy.33), calls=%async_computation | async-start | bytes 7340032 | tf_op jit(solution)/shard_map/all_to_all | solution.py:45
  407.6 90.1 %all-to-all-start.2 = ((bf16[16,16,7168]{2,1,0:T(8,128)(2,1)}), bf16[16,16,7168]{2,1,0:T(8,128)(2,1)}, u32[]{:S(2)}, u32[]{:S(2)}) async-start(bf16[16,16,7168]{2,1,0:T(8,128)(2,1)} %copy.37), calls=%async_computation.3 | async-start | bytes 7340032 | tf_op jit(solution)/shard_map/all_to_all | solution.py:46
  415.5 166.9 %reduce-scatter.3.cloned.1.call-start = ((), (), s32[]{:S(2)}) async-start(), calls=%async_computation.7 | async-start | bytes 3899392 | tf_op jit(solution)/shard_map/reduce_scatter | solution.py:23
  415.5 3.9 copy-start.2
  504.0 163.6 %reduce-scatter.5.cloned.1.call-start = ((), (), s32[]{:S(2)}) async-start(), calls=%async_computation.9 | async-start | bytes 3899392 | tf_op jit(solution)/shard_map/reduce_scatter | solution.py:23
  504.1 2.8 copy-start.1
  509.8 0.7 copy-start.4
  584.2 85.2 %all-to-all-start.1 = ((bf16[16,16,448]{2,1,0:T(8,128)(2,1)}), bf16[16,16,448]{2,1,0:T(8,128)(2,1)S(1)}, u32[]{:S(2)}, u32[]{:S(2)}) async-start(bf16[16,16,448]{2,1,0:T(8,128)(2,1)} %bitcast.7), calls=%async_computation.2 | async-start | bytes 524288 | tf_op jit(solution)/shard_map/all_to_all | solution.py:26
  669.4 21.7 %all-to-all-start.3 = ((bf16[16,16,448]{2,1,0:T(8,128)(2,1)}), bf16[16,16,448]{2,1,0:T(8,128)(2,1)}, u32[]{:S(2)}, u32[]{:S(2)}) async-start(bf16[16,16,448]{2,1,0:T(8,128)(2,1)} %bitcast.11), calls=%async_computation.5 | async-start | bytes 524288 | tf_op jit(solution)/shard_map/all_to_all | solution.py:26
Sparse Core Ops, SparseCore 0:
  13.6 184.1 all-gather.2
  200.8 180.2 all-gather.4
  504.1 78.2 reduce-scatter.2
  585.9 81.6 reduce-scatter.4
where the time goes:
time: 704 us; the launch traced here: 702 us
  waiting for transfers between devices  545 us (77%)
  local copies, waits for them, and re-layouts  68.8 us (10%)
  starting transfers between devices  34.7 us (5%)
  matrix products  31.8 us (5%)
  between operations  13.9 us (2%)
  other arithmetic  7.78 us (1%)
    all_gather x1, waiting for transfers between devices, per_device(): lax.all_gather(picked_tokens, 'fsdp', axis=2, tiled=True)  180 us
    all_gather x1, waiting for transfers between devices, per_device(): lax.all_gather(picked_grads, 'fsdp', axis=2, tiled=True)  148 us
    reduce_scatter x2, waiting for transfers between devices, send_back(): lax.psum_scatter(term.astype(jnp.bfloat16), 'fsdp', scatter_dimension=1,...  141 us
    all_to_all x1, waiting for transfers between devices, per_device(): lax.all_to_all(wide_grads, 'ep', split_axis=0, concat_axis=0, tiled=True)  75.2 us
    all_gather x1, local copies, waits for them, and re-layouts, per_device(): lax.all_gather(picked_tokens, 'fsdp', axis=2, tiled=True)  26.9 us
    all_gather x1, local copies, waits for them, and re-layouts, per_device(): lax.all_gather(picked_grads, 'fsdp', axis=2, tiled=True)  26.5 us
    all_to_all x2, starting transfers between devices, send_back(): lax.all_to_all(to_slots(summed, experts, slot_count), 'ep', split_axis=0,...  18.8 us
  transfers between devices with their start and end apart: 8, of which 5 were waited for; matrix products, arithmetic and copies ran while one was open for 13% of the time, Pallas kernels for 0%

commit v1 on v0

--- a/solution.py
+++ b/solution.py
@@ -38,7 +38,15 @@
     weight = jnp.where(live_mask, gate_prob[:, 0, :], 0.0)
     picked_tokens, picked_grads = pick_rows(tokens, cotangent, row_index, live_mask, weight)
     wide_tokens, wide_grads = (
-        lax.all_gather(picked_tokens, "fsdp", axis=2, tiled=True),
+        jnp.concatenate(
+            lax.all_to_all(
+                jnp.stack([picked_tokens for _ in range(lax.axis_size("fsdp"))], 0),
+                axis_name="fsdp",
+                split_axis=0,
+                concat_axis=0,
+            ),
+            2,
+        ),
         lax.all_gather(picked_grads, "fsdp", axis=2, tiled=True),
     )
     rows_tokens, rows_grads = (

time: 704 us -> 558 us (0.79)
  waiting for transfers between devices: 545 us -> 397 us
  starting transfers between devices: 34.7 us -> 48.6 us
  local copies, waits for them, and re-layouts: 68.8 us -> 57.6 us
    all_gather x1 -> x0, waiting for transfers between devices: 180 us -> none  [per_device(): lax.all_gather(picked_tokens, 'fsdp', axis=2, tiled=True)]
    all_to_all x0 -> x1, waiting for transfers between devices: none -> 65.6 us  [per_device(): lax.all_to_all(jnp.stack([picked_tokens for _ in range(lax.axis_size('fsd...]
    all_gather x1, waiting for transfers between devices: 148 us -> 115 us  [per_device(): lax.all_gather(picked_grads, 'fsdp', axis=2, tiled=True)]
    all_gather x1 -> x0, local copies, waits for them, and re-layouts: 26.9 us -> none  [per_device(): lax.all_gather(picked_tokens, 'fsdp', axis=2, tiled=True)]
    reshape x0 -> x2, local copies, waits for them, and re-layouts: none -> 15 us  [per_device(): jnp.concatenate(lax.all_to_all(jnp.stack([picked_tokens for _ in range(la...]
    all_to_all x0 -> x1, starting transfers between devices: none -> 7.76 us  [per_device(): lax.all_to_all(jnp.stack([picked_tokens for _ in range(lax.axis_size('fsd...]
  transfers between devices with their start and end apart: 8 -> 8, of which waited for: 5 -> 5; matrix products, arithmetic and copies ran while one was open for 13% -> 14% of each run, Pallas kernels for 0% -> 0%
where the time goes in v1:
time: 558 us; the launch traced here: 557 us
  waiting for transfers between devices  397 us (71%)
  local copies, waits for them, and re-layouts  57.6 us (10%)
  starting transfers between devices  48.6 us (9%)
  matrix products  31.8 us (6%)
  between operations  13.9 us (2%)
  other arithmetic  7.78 us (1%)
    reduce_scatter x2, waiting for transfers between devices, send_back(): lax.psum_scatter(term.astype(jnp.bfloat16), 'fsdp', scatter_dimension=1,...  141 us
    all_gather x1, waiting for transfers between devices, per_device(): lax.all_gather(picked_grads, 'fsdp', axis=2, tiled=True)  115 us
    all_to_all x1, waiting for transfers between devices, per_device(): lax.all_to_all(wide_grads, 'ep', split_axis=0, concat_axis=0, tiled=True)  75 us
    all_to_all x1, waiting for transfers between devices, per_device(): lax.all_to_all(jnp.stack([picked_tokens for _ in range(lax.axis_size('fsd...  65.6 us
    all_gather x1, local copies, waits for them, and re-layouts, per_device(): lax.all_gather(picked_grads, 'fsdp', axis=2, tiled=True)  26.5 us
    all_to_all x2, starting transfers between devices, send_back(): lax.all_to_all(to_slots(summed, experts, slot_count), 'ep', split_axis=0,...  18.7 us
    reshape x2, local copies, waits for them, and re-layouts, per_device(): jnp.concatenate(lax.all_to_all(jnp.stack([picked_tokens for _ in range(la...  15 us
    all_to_all x1, starting transfers between devices, per_device(): lax.all_to_all(wide_tokens, 'ep', split_axis=0, concat_axis=0, tiled=True)  13.9 us
  transfers between devices with their start and end apart: 8, of which 5 were waited for; matrix products, arithmetic and copies ran while one was open for 14% of the time, Pallas kernels for 0%

profile of v1, /device:TPU:1, one launch (start us, length us, event | category | flops | bytes accessed | tf_op | source)
XLA Modules:
  0.0 556.8 jit_solution(7177601298227461966)
XLA Ops:
  7.2 0.9 reshape_squeeze.7
  8.1 0.7 iota_compare_fusion
  8.8 0.1 lt.41
  8.9 1.2 copy.31
  10.2 1.2 gather_fusion
  11.3 0.1 select_select_fusion
  11.5 2.6 stack.3
  14.1 7.8 %all-to-all-start = ((bf16[16,16,16,448]{3,2,1,0:T(8,128)(2,1)}), bf16[16,16,16,448]{3,2,1,0:T(8,128)(2,1)}, u32[]{:S(2)}, u32[]{:S(2)}) async-start(bf16[16,16,16,448]{3,2,1,0:T(8,128)(2,1)} %stack.3), calls=%async_computation | async-start | bytes 8388608 | tf_op jit(solution)/shard_map/all_to_all | solution.py:42
  21.9 0.5 broadcast.75
  22.4 0.7 reduce.9
  23.1 0.1 squeeze.12
  23.2 0.2 copy.34
  23.4 1.2 gather_fusion.1
  24.5 0.1 multiply_convert_fusion
  24.7 1.9 copy.35
  26.6 65.6 %all-to-all-done = bf16[16,16,16,448]{3,2,1,0:T(8,128)(2,1)} async-done(((bf16[16,16,16,448]{3,2,1,0:T(8,128)(2,1)}), bf16[16,16,16,448]{3,2,1,0:T(8,128)(2,1)}, u32[]{:S(2)}, u32[]{:S(2)}) %all-to-all-start) | async-done | bytes 3670048 | tf_op jit(solution)/shard_map/all_to_all | solution.py:42
  92.3 7.1 %copy.32 = bf16[16,16,16,448]{3,2,1,0:T(8,128)(2,1)} copy(bf16[16,16,16,448]{3,1,0,2:T(8,128)(2,1)} %bitcast.3) | data formatting | bytes 7340032 | tf_op jit(solution)/shard_map/reshape | solution.py:41
  99.3 7.9 %reshape.102 = bf16[16,16,7168]{2,1,0:T(8,128)(2,1)} reshape(bf16[16,16,16,448]{3,2,1,0:T(8,128)(2,1)} %copy.32) | data formatting | bytes 7340032 | tf_op jit(solution)/shard_map/reshape | solution.py:41
  107.3 13.9 %all-to-all-start.1 = ((bf16[16,16,7168]{2,1,0:T(8,128)(2,1)}), bf16[16,16,7168]{2,1,0:T(8,128)(2,1)}, u32[]{:S(2)}, u32[]{:S(2)}) async-start(bf16[16,16,7168]{2,1,0:T(8,128)(2,1)} %reshape.102), calls=%async_computation.1 | async-start | bytes 7340032 | tf_op jit(solution)/shard_map/all_to_all | solution.py:53
  121.2 115.2 %all-gather.2.cloned.1.call-done = bf16[16,16,7168]{1,0,2:T(8,128)(2,1)} async-done(((bf16[16,16,448]{1,0,2:T(8,128)(2,1)}), bf16[16,16,7168]{1,0,2:T(8,128)(2,1)}) %all-gather.2.cloned.1.call-update) | async-done | bytes 3670032 | tf_op jit(solution)/shard_map/all_gather | solution.py:50
  236.4 26.5 %copy.36 = bf16[16,16,7168]{2,1,0:T(8,128)(2,1)} copy(bf16[16,16,7168]{1,0,2:T(8,128)(2,1)} %all-gather.2.cloned.1.call-done) | data formatting | bytes 7340032 | tf_op jit(solution)/shard_map/all_gather | solution.py:50
  262.9 7.9 %all-to-all-start.3 = ((bf16[16,16,7168]{2,1,0:T(8,128)(2,1)}), bf16[16,16,7168]{2,1,0:T(8,128)(2,1)}, u32[]{:S(2)}, u32[]{:S(2)}) async-start(bf16[16,16,7168]{2,1,0:T(8,128)(2,1)} %copy.36), calls=%async_computation.4 | async-start | bytes 7340032 | tf_op jit(solution)/shard_map/all_to_all | solution.py:54
  270.7 0.2 reduce-scatter.3.cloned.1.call-start
  271.0 3.8 fusion.8
  274.8 3.2 fusion.12
  278.0 75.0 %all-to-all-done.3 = bf16[16,16,7168]{2,1,0:T(8,128)(2,1)} async-done(((bf16[16,16,7168]{2,1,0:T(8,128)(2,1)}), bf16[16,16,7168]{2,1,0:T(8,128)(2,1)}, u32[]{:S(2)}, u32[]{:S(2)}) %all-to-all-start.3) | async-done | bytes 3670048 | tf_op jit(solution)/shard_map/all_to_all | solution.py:54
  353.0 3.1 multiply_convert_fusion.1
  356.2 3.1 convolution_convert_fusion
  359.3 2.7 fusion.10
  362.1 2.9 fusion
  365.1 0.5 broadcast.74
  365.6 0.2 copy-done.4
  365.7 0.7 reduce.8
  366.4 0.1 reshape_squeeze.6
  366.5 71.1 %reduce-scatter.3.cloned.1.call-done = bf16[256,448]{0,1:T(8,128)(2,1)} async-done(((bf16[256,7168]{0,1:T(8,128)(2,1)}), bf16[256,448]{0,1:T(8,128)(2,1)}) %reduce-scatter.3.cloned.1.call-update) | async-done | bytes 229392 | tf_op jit(solution)/shard_map/reduce_scatter | solution.py:23
  437.6 1.8 copy.33
  439.4 9.4 %all-to-all-start.2 = ((bf16[16,16,448]{2,1,0:T(8,128)(2,1)}), bf16[16,16,448]{2,1,0:T(8,128)(2,1)S(1)}, u32[]{:S(2)}, u32[]{:S(2)}) async-start(bf16[16,16,448]{2,1,0:T(8,128)(2,1)} %bitcast.8), calls=%async_computation.3 | async-start | bytes 524288 | tf_op jit(solution)/shard_map/all_to_all | solution.py:26
  448.7 4.0 fusion.3
  452.7 70.2 %reduce-scatter.5.cloned.1.call-done = bf16[256,448]{0,1:T(8,128)(2,1)} async-done(((bf16[256,7168]{0,1:T(8,128)(2,1)}), bf16[256,448]{0,1:T(8,128)(2,1)}) %reduce-scatter.5.cloned.1.call-update) | async-done | bytes 229392 | tf_op jit(solution)/shard_map/reduce_scatter | solution.py:23
  522.9 1.8 copy.37
  524.6 9.4 %all-to-all-start.4 = ((bf16[16,16,448]{2,1,0:T(8,128)(2,1)}), bf16[16,16,448]{2,1,0:T(8,128)(2,1)}, u32[]{:S(2)}, u32[]{:S(2)}) async-start(bf16[16,16,448]{2,1,0:T(8,128)(2,1)} %bitcast.12), calls=%async_computation.6 | async-start | bytes 524288 | tf_op jit(solution)/shard_map/all_to_all | solution.py:26
  534.0 4.4 fusion.2
  538.5 4.4 fusion.1
  542.9 2.4 scatter_custom_fusion
  545.3 0.1 convert_element_type.56
  545.4 1.0 copy.38
  546.4 2.8 scatter_custom_fusion.1
  549.3 1.0 copy.39
  (25 shorter events, 0.3 us)
Async XLA Ops:
  7.2 345.8 %copy-start = (bf16[1,128,7168]{2,1,0:T(8,128)(2,1)S(1)}, bf16[1,128,7168]{2,1,0:T(8,128)(2,1)}, u32[]{:S(2)}) copy-start(bf16[1,128,7168]{2,1,0:T(8,128)(2,1)} %param.14) | copy-start | bytes 5505028
  14.1 8.3 %copy-start.5 = (f32[16,1,16]{2,1,0:T(1,128)S(1)}, f32[16,1,16]{2,1,0:T(1,128)}, u32[]{:S(2)}) copy-start(f32[16,1,16]{2,1,0:T(1,128)} %param.17) | copy-start | bytes 3076
  14.1 9.1 %copy-start.3 = (bf16[512,448]{0,1:T(8,128)(2,1)S(1)}, bf16[512,448]{0,1:T(8,128)(2,1)}, u32[]{:S(2)}) copy-start(bf16[512,448]{0,1:T(8,128)(2,1)} %param.11) | copy-start | bytes 1376260
  14.1 78.2 %all-to-all-start = ((bf16[16,16,16,448]{3,2,1,0:T(8,128)(2,1)}), bf16[16,16,16,448]{3,2,1,0:T(8,128)(2,1)}, u32[]{:S(2)}, u32[]{:S(2)}) async-start(bf16[16,16,16,448]{3,2,1,0:T(8,128)(2,1)} %stack.3), calls=%async_computation | async-start | bytes 8388608 | tf_op jit(solution)/shard_map/all_to_all | solution.py:42
  21.8 214.5 %all-gather.2.cloned.1.call-start = ((), (), s32[]{:S(2)}) async-start(), calls=%async_computation.8 | async-start | bytes 31195136 | tf_op jit(solution)/shard_map/all_gather | solution.py:50
  107.3 155.6 %all-to-all-start.1 = ((bf16[16,16,7168]{2,1,0:T(8,128)(2,1)}), bf16[16,16,7168]{2,1,0:T(8,128)(2,1)}, u32[]{:S(2)}, u32[]{:S(2)}) async-start(bf16[16,16,7168]{2,1,0:T(8,128)(2,1)} %reshape.102), calls=%async_computation.1 | async-start | bytes 7340032 | tf_op jit(solution)/shard_map/all_to_all | solution.py:53
  262.9 90.1 %all-to-all-start.3 = ((bf16[16,16,7168]{2,1,0:T(8,128)(2,1)}), bf16[16,16,7168]{2,1,0:T(8,128)(2,1)}, u32[]{:S(2)}, u32[]{:S(2)}) async-start(bf16[16,16,7168]{2,1,0:T(8,128)(2,1)} %copy.36), calls=%async_computation.4 | async-start | bytes 7340032 | tf_op jit(solution)/shard_map/all_to_all | solution.py:54
  270.7 166.8 %reduce-scatter.3.cloned.1.call-start = ((), (), s32[]{:S(2)}) async-start(), calls=%async_computation.7 | async-start | bytes 3899392 | tf_op jit(solution)/shard_map/reduce_scatter | solution.py:23
  271.0 3.9 copy-start.2
  359.3 163.6 %reduce-scatter.5.cloned.1.call-start = ((), (), s32[]{:S(2)}) async-start(), calls=%async_computation.9 | async-start | bytes 3899392 | tf_op jit(solution)/shard_map/reduce_scatter | solution.py:23
  359.3 2.8 copy-start.1
  365.0 0.7 copy-start.4
  439.4 85.3 %all-to-all-start.2 = ((bf16[16,16,448]{2,1,0:T(8,128)(2,1)}), bf16[16,16,448]{2,1,0:T(8,128)(2,1)S(1)}, u32[]{:S(2)}, u32[]{:S(2)}) async-start(bf16[16,16,448]{2,1,0:T(8,128)(2,1)} %bitcast.8), calls=%async_computation.3 | async-start | bytes 524288 | tf_op jit(solution)/shard_map/all_to_all | solution.py:26
  524.6 21.7 %all-to-all-start.4 = ((bf16[16,16,448]{2,1,0:T(8,128)(2,1)}), bf16[16,16,448]{2,1,0:T(8,128)(2,1)}, u32[]{:S(2)}, u32[]{:S(2)}) async-start(bf16[16,16,448]{2,1,0:T(8,128)(2,1)} %bitcast.12), calls=%async_computation.6 | async-start | bytes 524288 | tf_op jit(solution)/shard_map/all_to_all | solution.py:26
Sparse Core Ops, SparseCore 0:
  26.7 209.5 all-gather.1
  359.4 78.1 reduce-scatter.2
  441.2 81.5 reduce-scatter.4
